TPU v7x, 32 devices: a whole 2x2x4 slice. The times are simulated.
32 devices in a mesh: groups: 2 (over x), pb: 16 (over z, y, core).
Axes of the slice: x: 2, y: 2, z: 4, core: 2. Of those that a mesh axis runs over, the one named last changes fastest.
Arguments:
- eigvec: bfloat16 [8192, 2592], P(('groups', 'pb')), parts along dimension 0, may hold values from -0.69921875 to 0.69921875
- omega: bfloat16 [8192, 36], P(('groups', 'pb')), parts along dimension 0, may hold values from 0.5 to 4
- phi: bfloat16 [36, 36, 36], replicated, may hold values from -6 to 6
- send_rows: int32 [32, 32], P(('groups', 'pb')), parts along dimension 0, may hold values from 0 to 255
- local_q: int32 [512], P(('groups', 'pb')), parts along dimension 0, may hold values from 0 to 255
- partner_q: int32 [512], P(('groups', 'pb')), parts along dimension 0, may hold values from 0 to 255
- slot_ref: int32 [512], P(('groups', 'pb')), parts along dimension 0, may hold values from 0 to 31, as said below
- tri_count: int32 [32], P(('groups', 'pb')), parts along dimension 0, may hold values from 8 to 16, as said below
Outputs:
- rates: float32 [36, 8192], P(None, ('groups', 'pb')), parts along dimension 1
There are 2 independent parts, one for each index of `groups`. A program takes and returns all parts, laid end to end along the dimension named above; an argument that names none is the same for every part. Nothing has to cross between parts.
Inputs may be any that keep to these rules, and one draw needn't show every extreme that they name: slot_ref of a live triplet of device p names an owner o and a slot s below the number of slots that o fills for p, which is 1 to 2; each device receives 2 filled slots from some owner. `tri_count`: exactly one device has 16 live triplets; live triplets come first.
All inputs are finite; a program needn't handle non-finite values.
Results may differ from a plain program's by a relative error of at most 0.00048.
Values may be sent and summed in bfloat16 or wider, within the bound.
A program may use at most 128 MiB of HBM per device.

v0:
```python
import jax
import jax.numpy as jnp
from jax import lax
from jax.sharding import PartitionSpec as P

NB = 36
BLK = 16
smear_width = 0.5


def triplet_rates(
    phi, near_vec, partner_vec, far_vec, near_freq, partner_freq, far_freq, weight_mask
):
    y_real = jnp.einsum("abc,tnc->tabn", phi, far_vec[:, 0], preferred_element_type=jnp.float32)
    y_imag = -jnp.einsum("abc,tnc->tabn", phi, far_vec[:, 1], preferred_element_type=jnp.float32)
    y_real = y_real.astype(jnp.bfloat16)
    y_imag = y_imag.astype(jnp.bfloat16)
    part_real = partner_vec[:, 0]
    part_imag = partner_vec[:, 1]
    z_real = jnp.einsum(
        "tmb,tabn->tamn", part_real, y_real, preferred_element_type=jnp.float32
    ) - jnp.einsum("tmb,tabn->tamn", part_imag, y_imag, preferred_element_type=jnp.float32)
    z_imag = jnp.einsum(
        "tmb,tabn->tamn", part_real, y_imag, preferred_element_type=jnp.float32
    ) + jnp.einsum("tmb,tabn->tamn", part_imag, y_real, preferred_element_type=jnp.float32)
    z_real = z_real.astype(jnp.bfloat16)
    z_imag = z_imag.astype(jnp.bfloat16)
    near_real = near_vec[:, 0]
    near_imag = near_vec[:, 1]
    v_real = jnp.einsum(
        "tva,tamn->tvmn", near_real, z_real, preferred_element_type=jnp.float32
    ) - jnp.einsum("tva,tamn->tvmn", near_imag, z_imag, preferred_element_type=jnp.float32)
    v_imag = jnp.einsum(
        "tva,tamn->tvmn", near_real, z_imag, preferred_element_type=jnp.float32
    ) + jnp.einsum("tva,tamn->tvmn", near_imag, z_real, preferred_element_type=jnp.float32)
    power = v_real * v_real + v_imag * v_imag
    first = near_freq.astype(jnp.float32)[:, :, None, None]
    second = partner_freq.astype(jnp.float32)[:, None, :, None]
    third = far_freq.astype(jnp.float32)[:, None, None, :]
    offset = (first + second - third) / smear_width
    weight = jnp.exp(-offset * offset) / (first * second * third * NB)
    terms = power * weight * weight_mask[:, None, None, None]
    return (jnp.sum(terms, axis=(2, 3)), jnp.sum(terms, axis=(1, 2)))


def on_device(eigvec, omega, phi, send_rows, local_q, partner_q, slot_ref, tri_count):
    owned = eigvec.shape[0]
    outgoing = send_rows[0]
    sent_vec = jnp.take(eigvec, outgoing, axis=0)
    sent_freq = jnp.take(omega, outgoing, axis=0)
    far_vecs, far_freqs = (
        lax.all_to_all(sent_vec, "pb", split_axis=0, concat_axis=0, tiled=True),
        lax.all_to_all(sent_freq, "pb", split_axis=0, concat_axis=0, tiled=True),
    )
    live = tri_count[0]
    tri_slots = local_q.shape[0]
    empty = jnp.zeros((tri_slots, NB), jnp.float32)

    def one_block(block, carry):
        start = block * BLK
        weight_mask = (start + jnp.arange(BLK, dtype=jnp.int32) < live).astype(jnp.float32)
        near_vec = jnp.take(eigvec, local_q, axis=0).reshape(BLK, 2, NB, NB)
        partner_vec = jnp.take(eigvec, partner_q, axis=0).reshape(BLK, 2, NB, NB)
        far_vec = jnp.take(far_vecs, slot_ref, axis=0).reshape(BLK, 2, NB, NB)
        near_part, far_part = triplet_rates(
            phi,
            near_vec,
            partner_vec,
            far_vec,
            jnp.take(omega, local_q, axis=0),
            jnp.take(omega, partner_q, axis=0),
            jnp.take(far_freqs, slot_ref, axis=0),
            weight_mask,
        )
        return (near_part, far_part)

    upper = (live + BLK - 1) // BLK
    near_terms, far_terms = lax.fori_loop(0, upper, one_block, (empty, empty))
    by_slot = jnp.zeros((NB, outgoing.shape[0]), jnp.float32)
    by_slot = by_slot.at[:, slot_ref].add(far_terms.T)
    returned = lax.all_to_all(by_slot, "pb", split_axis=1, concat_axis=1, tiled=True)
    rates = jnp.zeros((NB, owned), jnp.float32)
    rates = rates.at[:, local_q].add(near_terms.T)
    rates = rates.at[:, outgoing].add(returned)
    return rates


def solution(mesh):
    in_specs = (
        P(("groups", "pb"), None),
        P(("groups", "pb"), None),
        P(),
        P(("groups", "pb"), None),
        P(("groups", "pb")),
        P(("groups", "pb")),
        P(("groups", "pb")),
        P(("groups", "pb")),
    )
    out_specs = P(None, ("groups", "pb"))
    return jax.shard_map(
        on_device, mesh=mesh, in_specs=in_specs, out_specs=out_specs, check_vma=False
    )
```

profile of v0, /device:TPU:0, one launch (start us, length us, event | category | flops | bytes accessed | tf_op | source)
XLA Modules:
  0.0 156.0 jit_solution(6795776041242217636)
XLA Ops:
  1.2 1.3 reduce.3
  4.7 7.4 %all-to-all-start.1 = ((bf16[16,2,36]{2,1,0:T(2,128)(2,1)}), bf16[16,2,36]{2,1,0:T(2,128)(2,1)S(1)}, u32[]{:S(2)}, u32[]{:S(2)}) async-start(bf16[16,2,36]{2,1,0:T(2,128)(2,1)} %broadcast_select_fusion.3), calls=%async_computation.1 | async-start | bytes 16384 | tf_op jit(solution)/shard_map/all_to_all | solution.py:53
  14.8 1.8 %copy.29 = bf16[256,2592]{1,0:T(8,128)(2,1)S(1)} copy(bf16[256,2592]{0,1:T(8,128)(2,1)} %param.14) | data formatting | bytes 2654208 | tf_op args[0]
  18.6 0.9 broadcast_select_fusion
  22.1 6.0 %all-to-all-start = ((bf16[16,2,2592]{2,1,0:T(2,128)(2,1)}), bf16[16,2,2592]{2,1,0:T(2,128)(2,1)S(1)}, u32[]{:S(2)}, u32[]{:S(2)}) async-start(bf16[16,2,2592]{2,1,0:T(2,128)(2,1)} %broadcast_select_fusion), calls=%async_computation | async-start | bytes 344064 | tf_op jit(solution)/shard_map/all_to_all | solution.py:52
  28.8 7.9 %all-to-all-done = bf16[16,2,2592]{2,1,0:T(2,128)(2,1)S(1)} async-done(((bf16[16,2,2592]{2,1,0:T(2,128)(2,1)}), bf16[16,2,2592]{2,1,0:T(2,128)(2,1)S(1)}, u32[]{:S(2)}, u32[]{:S(2)}) %all-to-all-start) | async-done | bytes 165920 | tf_op jit(solution)/shard_map/all_to_all | solution.py:52
  38.6 104.5 %while.15 = (s32[]{:T(128)}, f32[16,36]{1,0:T(8,128)}, f32[16,36]{1,0:T(8,128)}, s32[]{:T(128)}, s32[16]{0:T(128)}, /*index=5*/bf16[16,2592]{1,0:T(8,128)(2,1)S(...) while((s32[]{:T(128)}, f32[16,36]{1,0:T(8,128)}, ...), condition=%wide.region_3.6_spmd, body=%wide.region_0.5_spmd.sunk | while | flops 554730752 | bytes 99940664 | solution.py:78
  38.6 1.3 compare_convert_fusion.2
  41.5 5.2 %fusion.58 = bf16[16,36,36,36]{2,3,1,0:T(8,128)(2,1)} fusion(bf16[36,36,36]{2,1,0:T(8,128)(2,1)} %get-tuple-element.391, bf16[16,2,36,36]{3,2,0,1:T(8,128)(2,1)S(1)} %copy_select_fusion.2), kind=kOutput, calls=%fused_computation.19.clone.1 | convolution fusion | flops 55240704 | bytes 1750144 | tf_op jit(solution)/shard_map/while/body/abc,tnc->tabn/dot_general | solution.py:15
  46.8 2.7 %convolution_convert_fusion.2 = bf16[16,36,36,36]{3,1,2,0:T(8,128)(2,1)S(1)} fusion(bf16[36,36,36]{2,1,0:T(8,128)(2,1)} %get-tuple-element.391, bf16[16,2,36,36]{3,2,0,1:T(8,128)(2,1)S(1)} %copy_select_fusion.2), kind=kOutput, calls=%fused_computation.26.clone.1 | convolution fusion | flops 54494208 | bytes 1750144 | tf_op jit(solution)/shard_map/while/body/abc,tnc->tabn/dot_general | solution.py:14
  49.5 2.5 %copy-done = bf16[16,36,36,36]{3,1,2,0:T(8,128)(2,1)} copy-done((bf16[16,36,36,36]{3,1,2,0:T(8,128)(2,1)}, bf16[16,36,36,36]{3,1,2,0:T(8,128)(2,1)S(1)}, u32[]{:S(2)}) %copy-start) | copy-done | bytes 1493016 | tf_op jit(solution)/shard_map/while
  52.0 5.3 %fusion.61 = f32[16,36,36,36]{3,2,1,0:T(8,128)} fusion(bf16[16,36,36,36]{3,1,2,0:T(8,128)(2,1)S(1)} %convolution_convert_fusion.2, bf16[16,2,36,36]{3,2,1,0:T(8,128)(2,1)S(1)} %reshape.251), kind=kOutput, calls=%fused_computation.24.clone.1 | convolution fusion | flops 53747712 | bytes 9048064 | tf_op jit(solution)/shard_map/while/body/tmb,tabn->tamn/dot_general | solution.py:20
  57.3 10.2 %fusion.62 = bf16[16,36,36,36]{2,3,1,0:T(8,128)(2,1)} fusion(f32[16,36,36,36]{3,2,1,0:T(8,128)} %fusion.61, bf16[16,36,36,36]{2,3,1,0:T(8,128)(2,1)} %fusion.58, bf16[16,2,36,36]{3,2,1,0:T(8,128)(2,1)S(1)} %reshape.251), kind=kOutput, calls=%fused_computation.20.clone.1 | convolution fusion | flops 55240704 | bytes 6135808 | tf_op jit(solution)/shard_map/while/body/tmb,tabn->tamn/dot_general | solution.py:22
  67.5 9.9 %copy.52 = bf16[16,36,36,36]{1,3,2,0:T(8,128)(2,1)} copy(bf16[16,36,36,36]{2,3,1,0:T(8,128)(2,1)} %fusion.62) | data formatting | bytes 2985984 | tf_op jit(solution)/shard_map/while/body/convert_element_type | solution.py:26
  77.4 8.7 %fusion.57 = f32[16,36,36,36]{3,2,1,0:T(8,128)} fusion(bf16[16,36,36,36]{3,1,2,0:T(8,128)(2,1)} %copy-done, bf16[16,2,36,36]{3,2,1,0:T(8,128)(2,1)S(1)} %reshape.251), kind=kOutput, calls=%fused_computation.22.clone.1 | convolution fusion | flops 53747712 | bytes 4642816 | tf_op jit(solution)/shard_map/while/body/tmb,tabn->tamn/dot_general | solution.py:25
  86.1 10.3 %fusion.59 = bf16[16,36,36,36]{2,3,1,0:T(8,128)(2,1)} fusion(f32[16,36,36,36]{3,2,1,0:T(8,128)} %fusion.57, bf16[16,36,36,36]{2,3,1,0:T(8,128)(2,1)} %fusion.58, bf16[16,2,36,36]{3,2,1,0:T(8,128)(2,1)S(1)} %reshape.251), kind=kOutput, calls=%fused_computation.21.clone.1 | convolution fusion | flops 55240704 | bytes 6135808 | tf_op jit(solution)/shard_map/while/body/tmb,tabn->tamn/dot_general | solution.py:23
  96.4 9.9 %copy.51 = bf16[16,36,36,36]{1,3,2,0:T(8,128)(2,1)} copy(bf16[16,36,36,36]{2,3,1,0:T(8,128)(2,1)} %fusion.59) | data formatting | bytes 2985984 | tf_op jit(solution)/shard_map/while/body/convert_element_type | solution.py:27
  106.2 8.9 %fusion.64 = f32[16,36,36,36]{3,2,1,0:T(8,128)} fusion(bf16[16,36,36,36]{1,3,2,0:T(8,128)(2,1)} %copy.51, bf16[16,2,36,36]{3,2,1,0:T(8,128)(2,1)S(1)} %reshape.252), kind=kOutput, calls=%fused_computation.40.clone.1 | convolution fusion | flops 53747712 | bytes 4642816 | tf_op jit(solution)/shard_map/while/body/tva,tamn->tvmn/dot_general | solution.py:32
  115.1 5.2 %fusion.60 = f32[16,36,36,36]{3,2,1,0:T(8,128)} fusion(bf16[16,36,36,36]{1,3,2,0:T(8,128)(2,1)S(1)} %copy-done.1, bf16[16,2,36,36]{3,2,1,0:T(8,128)(2,1)S(1)} %reshape.252), kind=kOutput, calls=%fused_computation.38.clone.1 | convolution fusion | flops 53747712 | bytes 9048064 | tf_op jit(solution)/shard_map/while/body/tva,tamn->tvmn/dot_general | solution.py:33
  120.3 5.2 %fusion.63 = f32[16,36,36,36]{3,2,1,0:T(8,128)} fusion(bf16[16,36,36,36]{1,3,2,0:T(8,128)(2,1)S(1)} %bitcast.133, bf16[16,2,36,36]{3,2,1,0:T(8,128)(2,1)S(1)} %reshape.252), kind=kOutput, calls=%fused_computation.39.clone.1 | convolution fusion | flops 53747712 | bytes 9048064 | tf_op jit(solution)/shard_map/while/body/tva,tamn->tvmn/dot_general | solution.py:30
  125.5 17.6 %fusion.65 = (f32[16,36]{1,0:T(8,128)}, f32[16,36]{1,0:T(8,128)}) fusion(f32[16]{0:T(128)S(1)} %get-tuple-element.349, f32[16,36,36]{1,2,0:T(8,128)S(1)} %get-tuple-element.350, f32[16,36]{1,0:T(8,128)S(1)} %select_convert_fusion.2, f32[16,36,36]{1,2,0:T(8,128)S(1)} %get-tuple-element.352, f32[16,36,36,36]{3,2,1,0:T(8,128)} %fusion.60, ...), kind=kOutput, calls=%fused_computation.68.clone.1 | convolution fusion | flops 65690496 | bytes 11283456 | tf_op jit(solution)/shard_map/while/body/tva,tamn->tvmn/dot_general | solution.py:35
  143.2 1.4 scatter_custom_fusion.1
  144.5 3.5 %all-to-all-start.2 = ((f32[36,16,2]{0,2,1:T(2,128)}), f32[36,16,2]{0,2,1:T(2,128)S(1)}, u32[]{:S(2)}, u32[]{:S(2)}) async-start(f32[36,16,2]{0,2,1:T(2,128)} %bitcast.33), calls=%async_computation.2 | async-start | bytes 32768 | tf_op jit(solution)/shard_map/all_to_all | solution.py:81
  148.9 5.6 %all-to-all-done.2 = f32[36,16,2]{0,2,1:T(2,128)S(1)} async-done(((f32[36,16,2]{0,2,1:T(2,128)}), f32[36,16,2]{0,2,1:T(2,128)S(1)}, u32[]{:S(2)}, u32[]{:S(2)}) %all-to-all-start.2) | async-done | bytes 4640 | tf_op jit(solution)/shard_map/all_to_all | solution.py:81
  (57 shorter events, 16.5 us)
Async XLA Ops:
  0.7 1.8 %copy-start.2 = (s32[32]{0:T(128)}, s32[32]{0:T(128)S(1)}, u32[]{:S(2)}) copy-start(s32[32]{0:T(128)S(1)} %fusion.20) | copy-start | bytes 388
  4.7 17.4 %all-to-all-start.1 = ((bf16[16,2,36]{2,1,0:T(2,128)(2,1)}), bf16[16,2,36]{2,1,0:T(2,128)(2,1)S(1)}, u32[]{:S(2)}, u32[]{:S(2)}) async-start(bf16[16,2,36]{2,1,0:T(2,128)(2,1)} %broadcast_select_fusion.3), calls=%async_computation.1 | async-start | bytes 16384 | tf_op jit(solution)/shard_map/all_to_all | solution.py:53
  13.5 3.1 %copy-start.4 = (s32[16]{0:T(128)}, s32[16]{0:T(128)S(1)}, u32[]{:S(2)}) copy-start(s32[16]{0:T(128)S(1)} %compare_select_fusion.5) | copy-start | bytes 196
  20.3 18.4 %copy-start.5 = (s32[16]{0:T(128)}, s32[16]{0:T(128)S(1)}, u32[]{:S(2)}) copy-start(s32[16]{0:T(128)S(1)} %compare_select_fusion.3) | copy-start | bytes 196
  22.1 14.6 %all-to-all-start = ((bf16[16,2,2592]{2,1,0:T(2,128)(2,1)}), bf16[16,2,2592]{2,1,0:T(2,128)(2,1)S(1)}, u32[]{:S(2)}, u32[]{:S(2)}) async-start(bf16[16,2,2592]{2,1,0:T(2,128)(2,1)} %broadcast_select_fusion), calls=%async_computation | async-start | bytes 344064 | tf_op jit(solution)/shard_map/all_to_all | solution.py:52
  38.6 115.9 %copy-start.3 = (s32[32]{0:T(128)S(1)}, s32[32]{0:T(128)}, u32[]{:S(2)}) copy-start(s32[32]{0:T(128)} %copy-done.2) | copy-start | bytes 388
  49.5 2.5 %copy-start = (bf16[16,36,36,36]{3,1,2,0:T(8,128)(2,1)}, bf16[16,36,36,36]{3,1,2,0:T(8,128)(2,1)S(1)}, u32[]{:S(2)}) copy-start(bf16[16,36,36,36]{3,1,2,0:T(8,128)(2,1)S(1)} %convolution_convert_fusion.2) | copy-start | bytes 4478980 | tf_op jit(solution)/shard_map/while
  106.2 8.9 %copy-start.1 = (bf16[16,36,36,36]{1,3,2,0:T(8,128)(2,1)S(1)}, bf16[16,36,36,36]{1,3,2,0:T(8,128)(2,1)}, u32[]{:S(2)}) copy-start(bf16[16,36,36,36]{1,3,2,0:T(8,128)(2,1)} %copy.51) | copy-start | bytes 4478980 | tf_op jit(solution)/shard_map/while
  106.2 14.1 %slice-start = ((s8[5898240]{0:T(1024)(128)(4,1)}), s8[4194304]{0:T(1024)(128)(4,1)S(1)}, s32[]{:S(2)}) async-start(s8[5898240]{0:T(1024)(128)(4,1)} %bitcast.132), calls=%async_computation.3 | async-start | bytes 8388608 | tf_op jit(solution)/shard_map/while
  115.1 5.2 %slice-start.1 = ((s8[5898240]{0:T(1024)(128)(4,1)}), s8[1703936]{0:T(1024)(128)(4,1)S(1)}, s32[]{:S(2)}) async-start(s8[5898240]{0:T(1024)(128)(4,1)} %bitcast.132), calls=%async_computation.4 | async-start | bytes 3407872 | tf_op jit(solution)/shard_map/while
  144.5 10.0 %all-to-all-start.2 = ((f32[36,16,2]{0,2,1:T(2,128)}), f32[36,16,2]{0,2,1:T(2,128)S(1)}, u32[]{:S(2)}, u32[]{:S(2)}) async-start(f32[36,16,2]{0,2,1:T(2,128)} %bitcast.33), calls=%async_computation.2 | async-start | bytes 32768 | tf_op jit(solution)/shard_map/all_to_all | solution.py:81
where the time goes:
time: 157 us; the launch traced here: 156 us
  matrix products  79.3 us (51%)
  local copies, waits for them, and re-layouts  33.6 us (21%)
  starting transfers between devices  16.9 us (11%)
  waiting for transfers between devices  13.5 us (9%)
  other arithmetic  11.7 us (7%)
    dot_general x1, matrix products, triplet_rates(): jnp.einsum('tva,tamn->tvmn', near_imag, z_real, preferred_element_type=jn...  17.6 us
    dot_general x1, matrix products, triplet_rates(): jnp.einsum('tmb,tabn->tamn', part_real, y_imag, preferred_element_type=jn...  10.3 us
    dot_general x1, matrix products, triplet_rates(): jnp.einsum('tmb,tabn->tamn', part_imag, y_imag, preferred_element_type=jn...  10.2 us
    convert_element_type x1, local copies, waits for them, and re-layouts, triplet_rates(): z_imag = z_imag.astype(jnp.bfloat16)  9.87 us
    convert_element_type x1, local copies, waits for them, and re-layouts, triplet_rates(): z_real = z_real.astype(jnp.bfloat16)  9.85 us
    dot_general x1, matrix products, triplet_rates(): jnp.einsum('tva,tamn->tvmn', near_imag, z_imag, preferred_element_type=jn...  8.89 us
    dot_general x1, matrix products, triplet_rates(): jnp.einsum('tmb,tabn->tamn', part_imag, y_real, preferred_element_type=jn...  8.74 us
    all_to_all x1, waiting for transfers between devices, on_device(): lax.all_to_all(sent_vec, 'pb', split_axis=0, concat_axis=0, tiled=True)  7.9 us
  transfers between devices with their start and end apart: 3, of which 2 were waited for; matrix products, arithmetic and copies ran while one was open for 7% of the time, Pallas kernels for 0%

commit v1 on v0

--- a/solution.py
+++ b/solution.py
@@ -78,7 +78,10 @@
     near_terms, far_terms = lax.fori_loop(0, upper, one_block, (empty, empty))
     by_slot = jnp.zeros((NB, outgoing.shape[0]), jnp.float32)
     by_slot = by_slot.at[:, slot_ref].add(far_terms.T)
-    returned = lax.all_to_all(by_slot, "pb", split_axis=1, concat_axis=1, tiled=True)
+    returned = jnp.concatenate(
+        lax.all_to_all(jnp.stack(jnp.split(by_slot, lax.axis_size("pb"), axis=1)), "pb", 0, 0),
+        axis=1,
+    )
     rates = jnp.zeros((NB, owned), jnp.float32)
     rates = rates.at[:, local_q].add(near_terms.T)
     rates = rates.at[:, outgoing].add(returned)

time: 157 us -> 166 us (1.057)
  local copies, waits for them, and re-layouts: 33.6 us -> 42.7 us
    unnamed x11 -> x26, local copies, waits for them, and re-layouts: 3.18 us -> 11.6 us
where the time goes in v1:
time: 166 us; the launch traced here: 165 us
  matrix products  79.3 us (48%)
  local copies, waits for them, and re-layouts  42.7 us (26%)
  starting transfers between devices  16.9 us (10%)
  waiting for transfers between devices  13.5 us (8%)
  other arithmetic  11.3 us (7%)
    dot_general x1, matrix products, triplet_rates(): jnp.einsum('tva,tamn->tvmn', near_imag, z_real, preferred_element_type=jn...  17.6 us
    unnamed x26, local copies, waits for them, and re-layouts  11.6 us
    dot_general x1, matrix products, triplet_rates(): jnp.einsum('tmb,tabn->tamn', part_real, y_imag, preferred_element_type=jn...  10.3 us
    dot_general x1, matrix products, triplet_rates(): jnp.einsum('tmb,tabn->tamn', part_imag, y_imag, preferred_element_type=jn...  10.2 us
    convert_element_type x1, local copies, waits for them, and re-layouts, triplet_rates(): z_imag = z_imag.astype(jnp.bfloat16)  9.88 us
    convert_element_type x1, local copies, waits for them, and re-layouts, triplet_rates(): z_real = z_real.astype(jnp.bfloat16)  9.84 us
    dot_general x1, matrix products, triplet_rates(): jnp.einsum('tva,tamn->tvmn', near_imag, z_imag, preferred_element_type=jn...  8.89 us
    dot_general x1, matrix products, triplet_rates(): jnp.einsum('tmb,tabn->tamn', part_imag, y_real, preferred_element_type=jn...  8.74 us
  transfers between devices with their start and end apart: 3, of which 2 were waited for; matrix products, arithmetic and copies ran while one was open for 7% of the time, Pallas kernels for 0%

profile of v1, /device:TPU:0, one launch (start us, length us, event | category | flops | bytes accessed | tf_op | source)
XLA Modules:
  0.0 164.6 jit_solution(12559125890154862435)
XLA Ops:
  1.2 1.3 reduce.3
  2.6 0.9 copy.32
  4.7 7.4 %all-to-all-start.1 = ((bf16[16,2,36]{2,1,0:T(2,128)(2,1)}), bf16[16,2,36]{2,1,0:T(2,128)(2,1)S(1)}, u32[]{:S(2)}, u32[]{:S(2)}) async-start(bf16[16,2,36]{2,1,0:T(2,128)(2,1)} %broadcast_select_fusion.3), calls=%async_computation.1 | async-start | bytes 16384 | tf_op jit(solution)/shard_map/all_to_all | solution.py:53
  15.4 1.8 %copy.29 = bf16[256,2592]{1,0:T(8,128)(2,1)S(1)} copy(bf16[256,2592]{0,1:T(8,128)(2,1)} %param.14) | data formatting | bytes 2654208 | tf_op args[0]
  19.3 0.9 broadcast_select_fusion
  22.2 6.0 %all-to-all-start = ((bf16[16,2,2592]{2,1,0:T(2,128)(2,1)}), bf16[16,2,2592]{2,1,0:T(2,128)(2,1)S(1)}, u32[]{:S(2)}, u32[]{:S(2)}) async-start(bf16[16,2,2592]{2,1,0:T(2,128)(2,1)} %broadcast_select_fusion), calls=%async_computation | async-start | bytes 344064 | tf_op jit(solution)/shard_map/all_to_all | solution.py:52
  28.9 7.9 %all-to-all-done = bf16[16,2,2592]{2,1,0:T(2,128)(2,1)S(1)} async-done(((bf16[16,2,2592]{2,1,0:T(2,128)(2,1)}), bf16[16,2,2592]{2,1,0:T(2,128)(2,1)S(1)}, u32[]{:S(2)}, u32[]{:S(2)}) %all-to-all-start) | async-done | bytes 165920 | tf_op jit(solution)/shard_map/all_to_all | solution.py:52
  38.8 104.5 %while.15 = (s32[]{:T(128)}, f32[16,36]{1,0:T(8,128)}, f32[16,36]{1,0:T(8,128)}, s32[]{:T(128)}, s32[16]{0:T(128)}, /*index=5*/bf16[16,2592]{1,0:T(8,128)(2,1)S(...) while((s32[]{:T(128)}, f32[16,36]{1,0:T(8,128)}, ...), condition=%wide.region_3.6_spmd, body=%wide.region_0.5_spmd.sunk | while | flops 554730752 | bytes 99940664 | solution.py:78
  38.8 1.3 compare_convert_fusion.2
  41.7 5.2 %fusion.58 = bf16[16,36,36,36]{2,3,1,0:T(8,128)(2,1)} fusion(bf16[36,36,36]{2,1,0:T(8,128)(2,1)} %get-tuple-element.389, bf16[16,2,36,36]{3,2,0,1:T(8,128)(2,1)S(1)} %copy_select_fusion.2), kind=kOutput, calls=%fused_computation.19.clone.1 | convolution fusion | flops 55240704 | bytes 1750144 | tf_op jit(solution)/shard_map/while/body/abc,tnc->tabn/dot_general | solution.py:15
  46.9 2.7 %convolution_convert_fusion.2 = bf16[16,36,36,36]{3,1,2,0:T(8,128)(2,1)S(1)} fusion(bf16[36,36,36]{2,1,0:T(8,128)(2,1)} %get-tuple-element.389, bf16[16,2,36,36]{3,2,0,1:T(8,128)(2,1)S(1)} %copy_select_fusion.2), kind=kOutput, calls=%fused_computation.26.clone.1 | convolution fusion | flops 54494208 | bytes 1750144 | tf_op jit(solution)/shard_map/while/body/abc,tnc->tabn/dot_general | solution.py:14
  49.6 2.5 %copy-done = bf16[16,36,36,36]{3,1,2,0:T(8,128)(2,1)} copy-done((bf16[16,36,36,36]{3,1,2,0:T(8,128)(2,1)}, bf16[16,36,36,36]{3,1,2,0:T(8,128)(2,1)S(1)}, u32[]{:S(2)}) %copy-start) | copy-done | bytes 1493016 | tf_op jit(solution)/shard_map/while
  52.1 5.3 %fusion.61 = f32[16,36,36,36]{3,2,1,0:T(8,128)} fusion(bf16[16,36,36,36]{3,1,2,0:T(8,128)(2,1)S(1)} %convolution_convert_fusion.2, bf16[16,2,36,36]{3,2,1,0:T(8,128)(2,1)S(1)} %reshape.257), kind=kOutput, calls=%fused_computation.24.clone.1 | convolution fusion | flops 53747712 | bytes 9048064 | tf_op jit(solution)/shard_map/while/body/tmb,tabn->tamn/dot_general | solution.py:20
  57.4 10.2 %fusion.62 = bf16[16,36,36,36]{2,3,1,0:T(8,128)(2,1)} fusion(f32[16,36,36,36]{3,2,1,0:T(8,128)} %fusion.61, bf16[16,36,36,36]{2,3,1,0:T(8,128)(2,1)} %fusion.58, bf16[16,2,36,36]{3,2,1,0:T(8,128)(2,1)S(1)} %reshape.257), kind=kOutput, calls=%fused_computation.20.clone.1 | convolution fusion | flops 55240704 | bytes 6135808 | tf_op jit(solution)/shard_map/while/body/tmb,tabn->tamn/dot_general | solution.py:22
  67.7 9.8 %copy.52 = bf16[16,36,36,36]{1,3,2,0:T(8,128)(2,1)} copy(bf16[16,36,36,36]{2,3,1,0:T(8,128)(2,1)} %fusion.62) | data formatting | bytes 2985984 | tf_op jit(solution)/shard_map/while/body/convert_element_type | solution.py:26
  77.5 8.7 %fusion.57 = f32[16,36,36,36]{3,2,1,0:T(8,128)} fusion(bf16[16,36,36,36]{3,1,2,0:T(8,128)(2,1)} %copy-done, bf16[16,2,36,36]{3,2,1,0:T(8,128)(2,1)S(1)} %reshape.257), kind=kOutput, calls=%fused_computation.22.clone.1 | convolution fusion | flops 53747712 | bytes 4642816 | tf_op jit(solution)/shard_map/while/body/tmb,tabn->tamn/dot_general | solution.py:25
  86.2 10.3 %fusion.59 = bf16[16,36,36,36]{2,3,1,0:T(8,128)(2,1)} fusion(f32[16,36,36,36]{3,2,1,0:T(8,128)} %fusion.57, bf16[16,36,36,36]{2,3,1,0:T(8,128)(2,1)} %fusion.58, bf16[16,2,36,36]{3,2,1,0:T(8,128)(2,1)S(1)} %reshape.257), kind=kOutput, calls=%fused_computation.21.clone.1 | convolution fusion | flops 55240704 | bytes 6135808 | tf_op jit(solution)/shard_map/while/body/tmb,tabn->tamn/dot_general | solution.py:23
  96.5 9.9 %copy.51 = bf16[16,36,36,36]{1,3,2,0:T(8,128)(2,1)} copy(bf16[16,36,36,36]{2,3,1,0:T(8,128)(2,1)} %fusion.59) | data formatting | bytes 2985984 | tf_op jit(solution)/shard_map/while/body/convert_element_type | solution.py:27
  106.4 8.9 %fusion.64 = f32[16,36,36,36]{3,2,1,0:T(8,128)} fusion(bf16[16,36,36,36]{1,3,2,0:T(8,128)(2,1)} %copy.51, bf16[16,2,36,36]{3,2,1,0:T(8,128)(2,1)S(1)} %reshape.258), kind=kOutput, calls=%fused_computation.40.clone.1 | convolution fusion | flops 53747712 | bytes 4642816 | tf_op jit(solution)/shard_map/while/body/tva,tamn->tvmn/dot_general | solution.py:32
  115.3 5.2 %fusion.60 = f32[16,36,36,36]{3,2,1,0:T(8,128)} fusion(bf16[16,36,36,36]{1,3,2,0:T(8,128)(2,1)S(1)} %copy-done.1, bf16[16,2,36,36]{3,2,1,0:T(8,128)(2,1)S(1)} %reshape.258), kind=kOutput, calls=%fused_computation.38.clone.1 | convolution fusion | flops 53747712 | bytes 9048064 | tf_op jit(solution)/shard_map/while/body/tva,tamn->tvmn/dot_general | solution.py:33
  120.5 5.2 %fusion.63 = f32[16,36,36,36]{3,2,1,0:T(8,128)} fusion(bf16[16,36,36,36]{1,3,2,0:T(8,128)(2,1)S(1)} %bitcast.198, bf16[16,2,36,36]{3,2,1,0:T(8,128)(2,1)S(1)} %reshape.258), kind=kOutput, calls=%fused_computation.39.clone.1 | convolution fusion | flops 53747712 | bytes 9048064 | tf_op jit(solution)/shard_map/while/body/tva,tamn->tvmn/dot_general | solution.py:30
  125.6 17.6 %fusion.65 = (f32[16,36]{1,0:T(8,128)}, f32[16,36]{1,0:T(8,128)}) fusion(f32[16]{0:T(128)S(1)} %get-tuple-element.347, f32[16,36,36]{1,2,0:T(8,128)S(1)} %get-tuple-element.348, f32[16,36]{1,0:T(8,128)S(1)} %select_convert_fusion.2, f32[16,36,36]{1,2,0:T(8,128)S(1)} %get-tuple-element.350, f32[16,36,36,36]{3,2,1,0:T(8,128)} %fusion.60, ...), kind=kOutput, calls=%fused_computation.100.clone.1 | convolution fusion | flops 65690496 | bytes 11283456 | tf_op jit(solution)/shard_map/while/body/tva,tamn->tvmn/dot_general | solution.py:35
  153.1 3.5 %all-to-all-start.2 = ((f32[16,36,2]{1,2,0:T(2,128)}), f32[16,36,2]{1,2,0:T(2,128)S(1)}, u32[]{:S(2)}, u32[]{:S(2)}) async-start(f32[16,36,2]{1,2,0:T(2,128)} %constant_dynamic-update-slice_fusion), calls=%async_computation.2 | async-start | bytes 32768 | tf_op jit(solution)/shard_map/all_to_all | solution.py:82
  157.5 5.6 %all-to-all-done.2 = f32[16,36,2]{1,2,0:T(2,128)S(1)} async-done(((f32[16,36,2]{1,2,0:T(2,128)}), f32[16,36,2]{1,2,0:T(2,128)S(1)}, u32[]{:S(2)}, u32[]{:S(2)}) %all-to-all-start.2) | async-done | bytes 4640 | tf_op jit(solution)/shard_map/all_to_all | solution.py:82
  (74 shorter events, 25.6 us)
Async XLA Ops:
  0.7 1.8 %copy-start.2 = (s32[32]{0:T(128)}, s32[32]{0:T(128)S(1)}, u32[]{:S(2)}) copy-start(s32[32]{0:T(128)S(1)} %fusion.20) | copy-start | bytes 388
  4.7 17.5 %all-to-all-start.1 = ((bf16[16,2,36]{2,1,0:T(2,128)(2,1)}), bf16[16,2,36]{2,1,0:T(2,128)(2,1)S(1)}, u32[]{:S(2)}, u32[]{:S(2)}) async-start(bf16[16,2,36]{2,1,0:T(2,128)(2,1)} %broadcast_select_fusion.3), calls=%async_computation.1 | async-start | bytes 16384 | tf_op jit(solution)/shard_map/all_to_all | solution.py:53
  13.5 5.0 %copy-start.4 = (s32[16]{0:T(128)}, s32[16]{0:T(128)S(1)}, u32[]{:S(2)}) copy-start(s32[16]{0:T(128)S(1)} %compare_select_fusion.5) | copy-start | bytes 196
  21.0 17.8 %copy-start.5 = (s32[16]{0:T(128)}, s32[16]{0:T(128)S(1)}, u32[]{:S(2)}) copy-start(s32[16]{0:T(128)S(1)} %compare_select_fusion.3) | copy-start | bytes 196
  22.2 14.6 %all-to-all-start = ((bf16[16,2,2592]{2,1,0:T(2,128)(2,1)}), bf16[16,2,2592]{2,1,0:T(2,128)(2,1)S(1)}, u32[]{:S(2)}, u32[]{:S(2)}) async-start(bf16[16,2,2592]{2,1,0:T(2,128)(2,1)} %broadcast_select_fusion), calls=%async_computation | async-start | bytes 344064 | tf_op jit(solution)/shard_map/all_to_all | solution.py:52
  38.8 124.3 %copy-start.3 = (s32[32]{0:T(128)S(1)}, s32[32]{0:T(128)}, u32[]{:S(2)}) copy-start(s32[32]{0:T(128)} %copy-done.2) | copy-start | bytes 388
  49.6 2.5 %copy-start = (bf16[16,36,36,36]{3,1,2,0:T(8,128)(2,1)}, bf16[16,36,36,36]{3,1,2,0:T(8,128)(2,1)S(1)}, u32[]{:S(2)}) copy-start(bf16[16,36,36,36]{3,1,2,0:T(8,128)(2,1)S(1)} %convolution_convert_fusion.2) | copy-start | bytes 4478980 | tf_op jit(solution)/shard_map/while
  106.4 8.9 %copy-start.1 = (bf16[16,36,36,36]{1,3,2,0:T(8,128)(2,1)S(1)}, bf16[16,36,36,36]{1,3,2,0:T(8,128)(2,1)}, u32[]{:S(2)}) copy-start(bf16[16,36,36,36]{1,3,2,0:T(8,128)(2,1)} %copy.51) | copy-start | bytes 4478980 | tf_op jit(solution)/shard_map/while
  106.4 14.1 %slice-start = ((s8[5898240]{0:T(1024)(128)(4,1)}), s8[4194304]{0:T(1024)(128)(4,1)S(1)}, s32[]{:S(2)}) async-start(s8[5898240]{0:T(1024)(128)(4,1)} %bitcast.197), calls=%async_computation.3 | async-start | bytes 8388608 | tf_op jit(solution)/shard_map/while
  115.3 5.2 %slice-start.1 = ((s8[5898240]{0:T(1024)(128)(4,1)}), s8[1703936]{0:T(1024)(128)(4,1)S(1)}, s32[]{:S(2)}) async-start(s8[5898240]{0:T(1024)(128)(4,1)} %bitcast.197), calls=%async_computation.4 | async-start | bytes 3407872 | tf_op jit(solution)/shard_map/while
  153.1 10.0 %all-to-all-start.2 = ((f32[16,36,2]{1,2,0:T(2,128)}), f32[16,36,2]{1,2,0:T(2,128)S(1)}, u32[]{:S(2)}, u32[]{:S(2)}) async-start(f32[16,36,2]{1,2,0:T(2,128)} %constant_dynamic-update-slice_fusion), calls=%async_computation.2 | async-start | bytes 32768 | tf_op jit(solution)/shard_map/all_to_all | solution.py:82
